TPU v7x, 256 devices: a whole 4x4x8 slice. The times are simulated.
256 devices in a mesh: slab: 32 (over x, y, core), orb: 8 (over z).
Axes of the slice: x: 4, y: 4, z: 8, core: 2. Of those that a mesh axis runs over, the one named last changes fastest.
Arguments:
- orbitals: float32 [256, 65536], P('orb', 'slab'), may hold values from -6 to 6
- cell_matrices: bfloat16 [256, 512, 512], P('slab'), as said below
- connectivity: int32 [256, 512], P('slab'), may hold values from 0 to 2559, as said below
- face_lower: int32 [8192], P('slab'), may hold values from 0 to 2047, as said below
- face_upper: int32 [8192], P('slab'), may hold values from 0 to 2047, as said below
Outputs:
- orthonormal_orbitals: float32 [256, 65536], P('orb', 'slab')
Inputs may be any that keep to these rules, and one draw needn't show every extreme that they name: `connectivity`: each row names 512 distinct positions of its slab's extended numbering. `face_lower`: each slab's block of 256 entries names distinct own nodes; it shares no entry with the same slab's block of face_upper. `face_upper`: each slab's block of 256 entries names distinct own nodes; it shares no entry with the same slab's block of face_lower. `cell_matrices`: each cell matrix is symmetric.
All inputs are finite; a program needn't handle non-finite values.
Results may differ from a plain program's by a relative error of at most 0.023.
Values may be sent and summed in bfloat16 or wider, within the bound.
A program may use at most 64 MiB of HBM per device.

v0:
```python
import math
import jax
import jax.numpy as jnp
from jax import lax
from jax.sharding import PartitionSpec as P

CELL_NODES = 512
DEGREE = 4
FACE = 256


def extended_2(cells, sides, width):
    for axis, dim in sides:
        count = lax.axis_size(axis)
        ends = count - 1
        head = lax.slice_in_dim(cells, 0, width, axis=dim)
        tail = lax.slice_in_dim(cells, cells.shape[dim] - width, cells.shape[dim], axis=dim)
        cells = jnp.concatenate(
            [
                lax.ppermute(tail, axis, [(i, (i + 1) % count) for i in range(ends)]),
                cells,
                lax.ppermute(head, axis, [((i + 1) % count, i) for i in range(ends)]),
            ],
            axis=dim,
        )
    return cells


def partner_2(value, axis, distance):
    mask = 2**distance
    pairs = [(source, source ^ mask) for source in range(lax.axis_size(axis))]
    return lax.ppermute(value, axis, pairs)


def gram_of(matrix):
    return lax.dot_general(
        matrix,
        matrix,
        (((1,), (1,)), ((), ())),
        precision=lax.Precision.HIGHEST,
        preferred_element_type=jnp.float32,
    )


def forward_solve(factor, values):
    return lax.linalg.triangular_solve(factor, values, left_side=True, lower=True)


def three_parts(values):
    upper_part = values.astype(jnp.bfloat16)
    remain = values - upper_part.astype(jnp.float32)
    middle_part = remain.astype(jnp.bfloat16)
    lowest_part = (remain - middle_part.astype(jnp.float32)).astype(jnp.bfloat16)
    return jnp.concatenate([upper_part, middle_part, lowest_part], axis=0)


def spread_back(values, table):
    row_count = values.shape[0]
    stacked = lax.dot_general(
        three_parts(values), table, (((1,), (1,)), ((), ())), preferred_element_type=jnp.float32
    )
    return stacked[:row_count] + stacked[row_count : 2 * row_count] + stacked[2 * row_count :]


def apply_cells(wave_field, cell_matrices, connectivity, face_table):
    rounded = wave_field.astype(jnp.bfloat16)
    orb_count, node_count = rounded.shape
    face_rows = jnp.dot(rounded, face_table, preferred_element_type=jnp.float32).astype(
        jnp.bfloat16
    )
    bordered = extended_2(face_rows, (("slab", 1),), FACE)
    extended = jnp.concatenate([bordered[:, :FACE], rounded, bordered[:, 3 * FACE :]], axis=1)
    ext_count = extended.shape[1]
    positions = lax.broadcasted_iota(jnp.int32, (ext_count, CELL_NODES), 0)

    def add_cell(summed, inputs):
        cell_block, cell_row = inputs
        picker = (positions == cell_row[None, :]).astype(jnp.bfloat16)
        pieces = jnp.dot(extended, picker, preferred_element_type=jnp.float32).astype(jnp.bfloat16)
        cell_terms = jnp.dot(pieces, cell_block, preferred_element_type=jnp.float32)
        return (summed + spread_back(cell_terms, picker), None)

    summed, _ = lax.scan(
        add_cell, jnp.zeros((orb_count, ext_count), jnp.float32), (cell_matrices, connectivity)
    )
    returned = jnp.concatenate([summed[:, :FACE], summed[:, FACE + node_count :]], axis=1)
    received = extended_2(returned, (("slab", 1),), FACE)
    incoming = jnp.concatenate([received[:, :FACE], received[:, 3 * FACE :]], axis=1)
    return summed[:, FACE : FACE + node_count] + spread_back(incoming, face_table)


def per_device(orbitals, cell_matrices, connectivity, face_lower, face_upper):
    node_count = orbitals.shape[1]
    face_nodes = jnp.concatenate([face_lower, face_upper], axis=0)
    face_table = (
        lax.broadcasted_iota(jnp.int32, (node_count, face_nodes.shape[0]), 0) == face_nodes[None, :]
    ).astype(jnp.bfloat16)
    previous = orbitals
    current = apply_cells(orbitals, cell_matrices, connectivity, face_table)
    for degree_step in range(1, DEGREE):
        following = 2.0 * apply_cells(current, cell_matrices, connectivity, face_table) - previous
        previous, current = (current, following)
    block_rows = orbitals.shape[0]
    norm_scale = math.sqrt(orbitals.shape[1] * lax.axis_size("slab"))
    gathered = lax.all_gather(current.astype(jnp.bfloat16), "orb", axis=0, tiled=True).astype(
        current.dtype
    )
    factor = jnp.linalg.cholesky(gram_of(gathered))
    for level in range(lax.axis_size("slab").bit_length() - 1):
        partner = partner_2(factor.astype(jnp.bfloat16), "slab", level).astype(factor.dtype)
        factor = jnp.linalg.cholesky(gram_of(factor) + gram_of(partner))
    solved = forward_solve(factor, gathered) * norm_scale
    result = lax.dynamic_slice_in_dim(solved, lax.axis_index("orb") * block_rows, block_rows, 0)
    return result


def solution(mesh):
    in_specs = (P("orb", "slab"), P("slab", None, None), P("slab", None), P("slab"), P("slab"))
    out_specs = P("orb", "slab")
    return jax.shard_map(
        per_device, mesh=mesh, in_specs=in_specs, out_specs=out_specs, check_vma=False
    )
```

profile of v0, /device:TPU:2, one launch (start us, length us, event | category | flops | bytes accessed | tf_op | source)
XLA Modules:
  0.0 538.3 jit_solution(7230007769574144148)
XLA Ops:
  10.9 5.8 %collective-permute-start.1 = (bf16[32,256]{1,0:T(8,128)(2,1)S(1)}, bf16[32,256]{1,0:T(8,128)(2,1)S(1)}, u32[]{:S(2)}, u32[]{:S(2)}) collective-permute-start(bf16[32,256]{1,0:T(8,128)(2,1)S(1)} %get-tuple-element.343), channel_id=1, source_target_pairs={{8,0},{16,8},{24,16},{32,24},{40,32},{48,40},{56,48},{64,56},{72,6... | collective-permute-start | bytes 49160 | tf_op jit(solution)/shard_map/ppermute | solution.py:22
  18.1 33.1 %while.46 = (s32[]{:T(128)}, f32[32,2560]{1,0:T(8,128)S(1)}, s32[8,512]{1,0:T(8,128)}, bf16[32,2560]{1,0:T(8,128)(2,1)S(1)}, bf16[8,512,512]{2,1,0:T(8,128)(2,1)}, /*index=5*/s32[]{:T(128)}, s32[]{:T(128)}) while((s32[]{:T(128)}, f32[32,2560]{1,0:T(8,128)S(1)}, s32[8,512]{1,0:T(8,128)}, bf16[32,2560]{1,0:T(8,128)(2,1)S(1)}, ...), condition=%wide.region_1.2_spmd.clone, body=%wide.region_0.1_spmd.clone.sunk | while | flops 357007360 | bytes 3514971 | solution.py:83
  53.2 5.8 %collective-permute-start.3 = (f32[32,256]{1,0:T(8,128)S(1)}, f32[32,256]{1,0:T(8,128)S(1)}, u32[]{:S(2)}, u32[]{:S(2)}) collective-permute-start(f32[32,256]{1,0:T(8,128)S(1)} %get-tuple-element.298), channel_id=1, source_target_pairs={{8,0},{16,8},{24,16},{32,24},{40,32},{48,40},{56,48},{64,56},{72,6... | collective-permute-start | bytes 98312 | tf_op jit(solution)/shard_map/ppermute | solution.py:22
  64.3 5.8 %collective-permute-start.5 = (bf16[32,256]{1,0:T(8,128)(2,1)S(1)}, bf16[32,256]{1,0:T(8,128)(2,1)S(1)}, u32[]{:S(2)}, u32[]{:S(2)}) collective-permute-start(bf16[32,256]{1,0:T(8,128)(2,1)S(1)} %get-tuple-element.341), channel_id=1, source_target_pairs={{8,0},{16,8},{24,16},{32,24},{40,32},{48,40},{56,48},{64,56},{72,6... | collective-permute-start | bytes 49160 | tf_op jit(solution)/shard_map/ppermute | solution.py:22
  71.5 27.5 %while.47 = (s32[]{:T(128)}, f32[32,2560]{1,0:T(8,128)S(1)}, s32[8,512]{1,0:T(8,128)S(1)}, bf16[32,2560]{1,0:T(8,128)(2,1)S(1)}, bf16[8,512,512]{2,1,0:T(8,128)(2,1)}, /*index=5*/s32[]{:T(128)}, s32[]{:T(128)}) while((s32[]{:T(128)}, f32[32,2560]{1,0:T(8,128)S(1)}, s32[8,512]{1,0:T(8,128)S(1)}, bf16[32,2560]{1,0:T(8,128)(2,1)S(1)}, ...), condition=%wide.region_3.4_spmd.clone, body=%wide.region_2.3_spmd.clone.sunk | while | flops 357007360 | bytes 3514971 | solution.py:83
  101.0 5.8 %collective-permute-start.7 = (f32[32,256]{1,0:T(8,128)S(1)}, f32[32,256]{1,0:T(8,128)S(1)}, u32[]{:S(2)}, u32[]{:S(2)}) collective-permute-start(f32[32,256]{1,0:T(8,128)S(1)} %get-tuple-element.296), channel_id=1, source_target_pairs={{8,0},{16,8},{24,16},{32,24},{40,32},{48,40},{56,48},{64,56},{72,6... | collective-permute-start | bytes 98312 | tf_op jit(solution)/shard_map/ppermute | solution.py:22
  112.1 5.8 %collective-permute-start.9 = (bf16[32,256]{1,0:T(8,128)(2,1)S(1)}, bf16[32,256]{1,0:T(8,128)(2,1)S(1)}, u32[]{:S(2)}, u32[]{:S(2)}) collective-permute-start(bf16[32,256]{1,0:T(8,128)(2,1)S(1)} %get-tuple-element.339), channel_id=1, source_target_pairs={{8,0},{16,8},{24,16},{32,24},{40,32},{48,40},{56,48},{64,56},{72,6... | collective-permute-start | bytes 49160 | tf_op jit(solution)/shard_map/ppermute | solution.py:22
  119.3 27.5 %while.48 = (s32[]{:T(128)}, f32[32,2560]{1,0:T(8,128)S(1)}, s32[8,512]{1,0:T(8,128)S(1)}, bf16[32,2560]{1,0:T(8,128)(2,1)S(1)}, bf16[8,512,512]{2,1,0:T(8,128)(2,1)}, /*index=5*/s32[]{:T(128)}, s32[]{:T(128)}) while((s32[]{:T(128)}, f32[32,2560]{1,0:T(8,128)S(1)}, s32[8,512]{1,0:T(8,128)S(1)}, bf16[32,2560]{1,0:T(8,128)(2,1)S(1)}, ...), condition=%wide.region_5.6_spmd.clone, body=%wide.region_4.5_spmd.clone.sunk | while | flops 357007360 | bytes 3514971 | solution.py:83
  148.7 6.0 %collective-permute-start.11 = (f32[32,256]{1,0:T(8,128)S(1)}, f32[32,256]{1,0:T(8,128)S(1)}, u32[]{:S(2)}, u32[]{:S(2)}) collective-permute-start(f32[32,256]{1,0:T(8,128)S(1)} %get-tuple-element.294), channel_id=1, source_target_pairs={{8,0},{16,8},{24,16},{32,24},{40,32},{48,40},{56,48},{64,56},{72,6... | collective-permute-start | bytes 98312 | tf_op jit(solution)/shard_map/ppermute | solution.py:22
  159.8 5.8 %collective-permute-start.13 = (bf16[32,256]{1,0:T(8,128)(2,1)S(1)}, bf16[32,256]{1,0:T(8,128)(2,1)S(1)}, u32[]{:S(2)}, u32[]{:S(2)}) collective-permute-start(bf16[32,256]{1,0:T(8,128)(2,1)S(1)} %get-tuple-element.337), channel_id=1, source_target_pairs={{8,0},{16,8},{24,16},{32,24},{40,32},{48,40},{56,48},{64,56},{72,6... | collective-permute-start | bytes 49160 | tf_op jit(solution)/shard_map/ppermute | solution.py:22
  167.0 27.5 %while.49 = (s32[]{:T(128)}, f32[32,2560]{1,0:T(8,128)S(1)}, s32[8,512]{1,0:T(8,128)S(1)}, bf16[32,2560]{1,0:T(8,128)(2,1)S(1)}, bf16[8,512,512]{2,1,0:T(8,128)(2,1)}, /*index=5*/s32[]{:T(128)}, s32[]{:T(128)}) while((s32[]{:T(128)}, f32[32,2560]{1,0:T(8,128)S(1)}, s32[8,512]{1,0:T(8,128)S(1)}, bf16[32,2560]{1,0:T(8,128)(2,1)S(1)}, ...), condition=%wide.region_7.8_spmd.clone, body=%wide.region_6.7_spmd.clone.sunk | while | flops 357007360 | bytes 3514971 | solution.py:83
  205.5 41.9 %all-gather.2.cloned.1.call-done = bf16[256,2048]{1,0:T(8,128)(2,1)} async-done(((bf16[32,2048]{1,0:T(8,128)(2,1)}), bf16[256,2048]{1,0:T(8,128)(2,1)}) %all-gather.2.cloned.1.call-update) | async-done | bytes 1048592 | tf_op jit(solution)/shard_map/all_gather | solution.py:105
  249.7 11.7 %cholesky.298 = f32[128,128]{1,0:T(8,128)S(1)} custom-call(f32[128,128]{1,0:T(8,128)S(1)} %cholesky.498), custom_call_target="Cholesky" | custom-call | tf_op jit(solution)/shard_map/jit(cholesky)/cholesky | solution.py:108
  261.4 9.8 %custom-call.21 = f32[1,128,128]{1,2,0:T(8,128)S(1)} custom-call(f32[1,128,128]{2,1,0:T(8,128)S(1)} %get-tuple-element.323), custom_call_target="InvertDiagBlocksLowerTriangular" | custom-call | tf_op jit(solution)/shard_map/jit(cholesky)/cholesky | solution.py:108
  271.7 11.7 %cholesky.315 = f32[128,128]{1,0:T(8,128)S(1)} custom-call(f32[128,128]{1,0:T(8,128)S(1)} %convolution_subtract_fusion.1), custom_call_target="Cholesky" | custom-call | tf_op jit(solution)/shard_map/jit(cholesky)/cholesky | solution.py:108
  285.4 8.4 %collective-permute-start.16 = (bf16[256,256]{1,0:T(8,128)(2,1)S(1)}, bf16[256,256]{1,0:T(8,128)(2,1)S(1)}, u32[]{:S(2)}, u32[]{:S(2)}) collective-permute-start(bf16[256,256]{1,0:T(8,128)(2,1)S(1)} %fusion.143), channel_id=1, source_target_pairs={{0,8},{8,0},{16,24},{24,16},{32,40},{40,32},{48,56},{56,48},{64,72... | collective-permute-start | bytes 393224 | tf_op jit(solution)/shard_map/ppermute | solution.py:32
  295.5 11.7 %cholesky.332 = f32[128,128]{1,0:T(8,128)S(1)} custom-call(f32[128,128]{1,0:T(8,128)S(1)} %cholesky.501), custom_call_target="Cholesky" | custom-call | tf_op jit(solution)/shard_map/jit(cholesky)/cholesky | solution.py:111
  307.3 9.8 %custom-call.22 = f32[1,128,128]{1,2,0:T(8,128)S(1)} custom-call(f32[1,128,128]{2,1,0:T(8,128)S(1)} %get-tuple-element.319), custom_call_target="InvertDiagBlocksLowerTriangular" | custom-call | tf_op jit(solution)/shard_map/jit(cholesky)/cholesky | solution.py:111
  317.6 11.7 %cholesky.349 = f32[128,128]{1,0:T(8,128)S(1)} custom-call(f32[128,128]{1,0:T(8,128)S(1)} %slice_subtract_fusion.4), custom_call_target="Cholesky" | custom-call | tf_op jit(solution)/shard_map/jit(cholesky)/cholesky | solution.py:111
  338.1 11.7 %cholesky.366 = f32[128,128]{1,0:T(8,128)S(1)} custom-call(f32[128,128]{1,0:T(8,128)S(1)} %cholesky.504), custom_call_target="Cholesky" | custom-call | tf_op jit(solution)/shard_map/jit(cholesky)/cholesky | solution.py:111
  349.9 9.8 %custom-call.23 = f32[1,128,128]{1,2,0:T(8,128)S(1)} custom-call(f32[1,128,128]{2,1,0:T(8,128)S(1)} %get-tuple-element.315), custom_call_target="InvertDiagBlocksLowerTriangular" | custom-call | tf_op jit(solution)/shard_map/jit(cholesky)/cholesky | solution.py:111
  360.2 11.7 %cholesky.383 = f32[128,128]{1,0:T(8,128)S(1)} custom-call(f32[128,128]{1,0:T(8,128)S(1)} %slice_subtract_fusion.3), custom_call_target="Cholesky" | custom-call | tf_op jit(solution)/shard_map/jit(cholesky)/cholesky | solution.py:111
  381.8 11.7 %cholesky.400 = f32[128,128]{1,0:T(8,128)S(1)} custom-call(f32[128,128]{1,0:T(8,128)S(1)} %cholesky.507), custom_call_target="Cholesky" | custom-call | tf_op jit(solution)/shard_map/jit(cholesky)/cholesky | solution.py:111
  393.6 9.8 %custom-call.24 = f32[1,128,128]{1,2,0:T(8,128)S(1)} custom-call(f32[1,128,128]{2,1,0:T(8,128)S(1)} %get-tuple-element.311), custom_call_target="InvertDiagBlocksLowerTriangular" | custom-call | tf_op jit(solution)/shard_map/jit(cholesky)/cholesky | solution.py:111
  403.9 11.7 %cholesky.417 = f32[128,128]{1,0:T(8,128)S(1)} custom-call(f32[128,128]{1,0:T(8,128)S(1)} %slice_subtract_fusion.2), custom_call_target="Cholesky" | custom-call | tf_op jit(solution)/shard_map/jit(cholesky)/cholesky | solution.py:111
  423.8 11.7 %cholesky.434 = f32[128,128]{1,0:T(8,128)S(1)} custom-call(f32[128,128]{1,0:T(8,128)S(1)} %cholesky.510), custom_call_target="Cholesky" | custom-call | tf_op jit(solution)/shard_map/jit(cholesky)/cholesky | solution.py:111
  435.6 9.8 %custom-call.25 = f32[1,128,128]{1,2,0:T(8,128)S(1)} custom-call(f32[1,128,128]{2,1,0:T(8,128)S(1)} %get-tuple-element.307), custom_call_target="InvertDiagBlocksLowerTriangular" | custom-call | tf_op jit(solution)/shard_map/jit(cholesky)/cholesky | solution.py:111
  445.9 11.7 %cholesky.451 = f32[128,128]{1,0:T(8,128)S(1)} custom-call(f32[128,128]{1,0:T(8,128)S(1)} %slice_subtract_fusion.1), custom_call_target="Cholesky" | custom-call | tf_op jit(solution)/shard_map/jit(cholesky)/cholesky | solution.py:111
  467.4 11.7 %cholesky.468 = f32[128,128]{1,0:T(8,128)S(1)} custom-call(f32[128,128]{1,0:T(8,128)S(1)} %cholesky.513), custom_call_target="Cholesky" | custom-call | tf_op jit(solution)/shard_map/jit(cholesky)/cholesky | solution.py:111
  479.1 9.8 %custom-call.26 = f32[1,128,128]{1,2,0:T(8,128)S(1)} custom-call(f32[1,128,128]{2,1,0:T(8,128)S(1)} %get-tuple-element.303), custom_call_target="InvertDiagBlocksLowerTriangular" | custom-call | tf_op jit(solution)/shard_map/jit(cholesky)/cholesky | solution.py:111
  489.4 11.7 %cholesky.485 = f32[128,128]{1,0:T(8,128)S(1)} custom-call(f32[128,128]{1,0:T(8,128)S(1)} %slice_subtract_fusion), custom_call_target="Cholesky" | custom-call | tf_op jit(solution)/shard_map/jit(cholesky)/cholesky | solution.py:111
  507.8 19.7 %custom-call.11 = f32[2,128,128]{1,2,0:T(8,128)S(1)} custom-call(f32[2,128,128]{2,1,0:T(8,128)S(1)} %get-tuple-element.145), custom_call_target="InvertDiagBlocksLowerTriangular" | custom-call | tf_op jit(solution)/shard_map/triangular_solve | solution.py:46
  (302 shorter events, 208.9 us)
Async XLA Ops:
  6.5 240.9 %all-gather.2.cloned.1.call-start = ((), (), s32[]{:S(2)}) async-start(), calls=%async_computation | async-start | bytes 1179648 | tf_op jit(solution)/shard_map/all_gather | solution.py:105
  9.0 7.7 %collective-permute-start = (bf16[32,256]{1,0:T(8,128)(2,1)S(1)}, bf16[32,256]{1,0:T(8,128)(2,1)S(1)}, u32[]{:S(2)}, u32[]{:S(2)}) collective-permute-start(bf16[32,256]{1,0:T(8,128)(2,1)S(1)} %get-tuple-element.342), channel_id=1, source_target_pairs={{0,8},{8,16},{16,24},{24,32},{32,40},{40,48},{48,56},{56,64},{64,7... | collective-permute-start | bytes 49160 | tf_op jit(solution)/shard_map/ppermute | solution.py:20
  10.9 7.2 %collective-permute-start.1 = (bf16[32,256]{1,0:T(8,128)(2,1)S(1)}, bf16[32,256]{1,0:T(8,128)(2,1)S(1)}, u32[]{:S(2)}, u32[]{:S(2)}) collective-permute-start(bf16[32,256]{1,0:T(8,128)(2,1)S(1)} %get-tuple-element.343), channel_id=1, source_target_pairs={{8,0},{16,8},{24,16},{32,24},{40,32},{48,40},{56,48},{64,56},{72,6... | collective-permute-start | bytes 49160 | tf_op jit(solution)/shard_map/ppermute | solution.py:22
  51.3 20.2 %copy-start.2 = (s32[8,512]{1,0:T(8,128)S(1)}, s32[8,512]{1,0:T(8,128)}, u32[]{:S(2)}) copy-start(s32[8,512]{1,0:T(8,128)} %get-tuple-element.649) | copy-start | bytes 49156
  51.3 7.7 %collective-permute-start.2 = (f32[32,256]{1,0:T(8,128)S(1)}, f32[32,256]{1,0:T(8,128)S(1)}, u32[]{:S(2)}, u32[]{:S(2)}) collective-permute-start(f32[32,256]{1,0:T(8,128)S(1)} %get-tuple-element.299), channel_id=1, source_target_pairs={{0,8},{8,16},{16,24},{24,32},{32,40},{40,48},{48,56},{56,64},{64,7... | collective-permute-start | bytes 98312 | tf_op jit(solution)/shard_map/ppermute | solution.py:20
  53.2 7.3 %collective-permute-start.3 = (f32[32,256]{1,0:T(8,128)S(1)}, f32[32,256]{1,0:T(8,128)S(1)}, u32[]{:S(2)}, u32[]{:S(2)}) collective-permute-start(f32[32,256]{1,0:T(8,128)S(1)} %get-tuple-element.298), channel_id=1, source_target_pairs={{8,0},{16,8},{24,16},{32,24},{40,32},{48,40},{56,48},{64,56},{72,6... | collective-permute-start | bytes 98312 | tf_op jit(solution)/shard_map/ppermute | solution.py:22
  62.3 7.7 %collective-permute-start.4 = (bf16[32,256]{1,0:T(8,128)(2,1)S(1)}, bf16[32,256]{1,0:T(8,128)(2,1)S(1)}, u32[]{:S(2)}, u32[]{:S(2)}) collective-permute-start(bf16[32,256]{1,0:T(8,128)(2,1)S(1)} %get-tuple-element.340), channel_id=1, source_target_pairs={{0,8},{8,16},{16,24},{24,32},{32,40},{40,48},{48,56},{56,64},{64,7... | collective-permute-start | bytes 49160 | tf_op jit(solution)/shard_map/ppermute | solution.py:20
  64.3 7.2 %collective-permute-start.5 = (bf16[32,256]{1,0:T(8,128)(2,1)S(1)}, bf16[32,256]{1,0:T(8,128)(2,1)S(1)}, u32[]{:S(2)}, u32[]{:S(2)}) collective-permute-start(bf16[32,256]{1,0:T(8,128)(2,1)S(1)} %get-tuple-element.341), channel_id=1, source_target_pairs={{8,0},{16,8},{24,16},{32,24},{40,32},{48,40},{56,48},{64,56},{72,6... | collective-permute-start | bytes 49160 | tf_op jit(solution)/shard_map/ppermute | solution.py:22
  71.5 37.7 %copy-start.1 = (f32[32,2048]{1,0:T(8,128)S(1)}, f32[32,2048]{1,0:T(8,128)}, u32[]{:S(2)}) copy-start(f32[32,2048]{1,0:T(8,128)} %param.14) | copy-start | bytes 786436
  99.0 7.7 %collective-permute-start.6 = (f32[32,256]{1,0:T(8,128)S(1)}, f32[32,256]{1,0:T(8,128)S(1)}, u32[]{:S(2)}, u32[]{:S(2)}) collective-permute-start(f32[32,256]{1,0:T(8,128)S(1)} %get-tuple-element.297), channel_id=1, source_target_pairs={{0,8},{8,16},{16,24},{24,32},{32,40},{40,48},{48,56},{56,64},{64,7... | collective-permute-start | bytes 98312 | tf_op jit(solution)/shard_map/ppermute | solution.py:20
  101.0 7.3 %collective-permute-start.7 = (f32[32,256]{1,0:T(8,128)S(1)}, f32[32,256]{1,0:T(8,128)S(1)}, u32[]{:S(2)}, u32[]{:S(2)}) collective-permute-start(f32[32,256]{1,0:T(8,128)S(1)} %get-tuple-element.296), channel_id=1, source_target_pairs={{8,0},{16,8},{24,16},{32,24},{40,32},{48,40},{56,48},{64,56},{72,6... | collective-permute-start | bytes 98312 | tf_op jit(solution)/shard_map/ppermute | solution.py:22
  110.1 7.7 %collective-permute-start.8 = (bf16[32,256]{1,0:T(8,128)(2,1)S(1)}, bf16[32,256]{1,0:T(8,128)(2,1)S(1)}, u32[]{:S(2)}, u32[]{:S(2)}) collective-permute-start(bf16[32,256]{1,0:T(8,128)(2,1)S(1)} %get-tuple-element.338), channel_id=1, source_target_pairs={{0,8},{8,16},{16,24},{24,32},{32,40},{40,48},{48,56},{56,64},{64,7... | collective-permute-start | bytes 49160 | tf_op jit(solution)/shard_map/ppermute | solution.py:20
  112.1 7.2 %collective-permute-start.9 = (bf16[32,256]{1,0:T(8,128)(2,1)S(1)}, bf16[32,256]{1,0:T(8,128)(2,1)S(1)}, u32[]{:S(2)}, u32[]{:S(2)}) collective-permute-start(bf16[32,256]{1,0:T(8,128)(2,1)S(1)} %get-tuple-element.339), channel_id=1, source_target_pairs={{8,0},{16,8},{24,16},{32,24},{40,32},{48,40},{56,48},{64,56},{72,6... | collective-permute-start | bytes 49160 | tf_op jit(solution)/shard_map/ppermute | solution.py:22
  146.8 7.9 %collective-permute-start.10 = (f32[32,256]{1,0:T(8,128)S(1)}, f32[32,256]{1,0:T(8,128)S(1)}, u32[]{:S(2)}, u32[]{:S(2)}) collective-permute-start(f32[32,256]{1,0:T(8,128)S(1)} %get-tuple-element.295), channel_id=1, source_target_pairs={{0,8},{8,16},{16,24},{24,32},{32,40},{40,48},{48,56},{56,64},{64,7... | collective-permute-start | bytes 98312 | tf_op jit(solution)/shard_map/ppermute | solution.py:20
  148.7 7.3 %collective-permute-start.11 = (f32[32,256]{1,0:T(8,128)S(1)}, f32[32,256]{1,0:T(8,128)S(1)}, u32[]{:S(2)}, u32[]{:S(2)}) collective-permute-start(f32[32,256]{1,0:T(8,128)S(1)} %get-tuple-element.294), channel_id=1, source_target_pairs={{8,0},{16,8},{24,16},{32,24},{40,32},{48,40},{56,48},{64,56},{72,6... | collective-permute-start | bytes 98312 | tf_op jit(solution)/shard_map/ppermute | solution.py:22
  157.9 7.7 %collective-permute-start.12 = (bf16[32,256]{1,0:T(8,128)(2,1)S(1)}, bf16[32,256]{1,0:T(8,128)(2,1)S(1)}, u32[]{:S(2)}, u32[]{:S(2)}) collective-permute-start(bf16[32,256]{1,0:T(8,128)(2,1)S(1)} %get-tuple-element.336), channel_id=1, source_target_pairs={{0,8},{8,16},{16,24},{24,32},{32,40},{40,48},{48,56},{56,64},{64,7... | collective-permute-start | bytes 49160 | tf_op jit(solution)/shard_map/ppermute | solution.py:20
  159.8 7.2 %collective-permute-start.13 = (bf16[32,256]{1,0:T(8,128)(2,1)S(1)}, bf16[32,256]{1,0:T(8,128)(2,1)S(1)}, u32[]{:S(2)}, u32[]{:S(2)}) collective-permute-start(bf16[32,256]{1,0:T(8,128)(2,1)S(1)} %get-tuple-element.337), channel_id=1, source_target_pairs={{8,0},{16,8},{24,16},{32,24},{40,32},{48,40},{56,48},{64,56},{72,6... | collective-permute-start | bytes 49160 | tf_op jit(solution)/shard_map/ppermute | solution.py:22
  194.5 7.7 %collective-permute-start.14 = (f32[32,256]{1,0:T(8,128)S(1)}, f32[32,256]{1,0:T(8,128)S(1)}, u32[]{:S(2)}, u32[]{:S(2)}) collective-permute-start(f32[32,256]{1,0:T(8,128)S(1)} %get-tuple-element.293), channel_id=1, source_target_pairs={{0,8},{8,16},{16,24},{24,32},{32,40},{40,48},{48,56},{56,64},{64,7... | collective-permute-start | bytes 98312 | tf_op jit(solution)/shard_map/ppermute | solution.py:20
  196.4 7.3 %collective-permute-start.15 = (f32[32,256]{1,0:T(8,128)S(1)}, f32[32,256]{1,0:T(8,128)S(1)}, u32[]{:S(2)}, u32[]{:S(2)}) collective-permute-start(f32[32,256]{1,0:T(8,128)S(1)} %get-tuple-element.292), channel_id=1, source_target_pairs={{8,0},{16,8},{24,16},{32,24},{40,32},{48,40},{56,48},{64,56},{72,6... | collective-permute-start | bytes 98312 | tf_op jit(solution)/shard_map/ppermute | solution.py:22
  285.4 9.7 %collective-permute-start.16 = (bf16[256,256]{1,0:T(8,128)(2,1)S(1)}, bf16[256,256]{1,0:T(8,128)(2,1)S(1)}, u32[]{:S(2)}, u32[]{:S(2)}) collective-permute-start(bf16[256,256]{1,0:T(8,128)(2,1)S(1)} %fusion.143), channel_id=1, source_target_pairs={{0,8},{8,0},{16,24},{24,16},{32,40},{40,32},{48,56},{56,48},{64,72... | collective-permute-start | bytes 393224 | tf_op jit(solution)/shard_map/ppermute | solution.py:32
  331.8 5.8 %collective-permute-start.17 = (bf16[256,256]{1,0:T(8,128)(2,1)S(1)}, bf16[256,256]{1,0:T(8,128)(2,1)S(1)}, u32[]{:S(2)}, u32[]{:S(2)}) collective-permute-start(bf16[256,256]{1,0:T(8,128)(2,1)S(1)} %fusion.145), channel_id=1, source_target_pairs={{0,16},{8,24},{16,0},{24,8},{32,48},{40,56},{48,32},{56,40},{64,80... | collective-permute-start | bytes 393224 | tf_op jit(solution)/shard_map/ppermute | solution.py:32
  374.4 7.0 %collective-permute-start.18 = (bf16[256,256]{1,0:T(8,128)(2,1)S(1)}, bf16[256,256]{1,0:T(8,128)(2,1)S(1)}, u32[]{:S(2)}, u32[]{:S(2)}) collective-permute-start(bf16[256,256]{1,0:T(8,128)(2,1)S(1)} %fusion.147), channel_id=1, source_target_pairs={{0,32},{8,40},{16,48},{24,56},{32,0},{40,8},{48,16},{56,24},{64,96... | collective-permute-start | bytes 393224 | tf_op jit(solution)/shard_map/ppermute | solution.py:32
  418.2 5.2 collective-permute-start.19
  423.6 103.9 %copy-start = (bf16[256,2048]{1,0:T(8,128)(2,1)S(1)}, bf16[256,2048]{1,0:T(8,128)(2,1)}, u32[]{:S(2)}) copy-start(bf16[256,2048]{1,0:T(8,128)(2,1)} %all-gather.2.cloned.1.call-done) | copy-start | bytes 3145732
  460.2 6.8 %collective-permute-start.20 = (bf16[256,256]{1,0:T(8,128)(2,1)S(1)}, bf16[256,256]{1,0:T(8,128)(2,1)S(1)}, u32[]{:S(2)}, u32[]{:S(2)}) collective-permute-start(bf16[256,256]{1,0:T(8,128)(2,1)S(1)} %fusion.151), channel_id=1, source_target_pairs={{0,128},{8,136},{16,144},{24,152},{32,160},{40,168},{48,176},{56,1... | collective-permute-start | bytes 393224 | tf_op jit(solution)/shard_map/ppermute | solution.py:32
Sparse Core Ops, SparseCore 0:
  205.6 41.7 all-gather.1
where the time goes:
time: 549 us; the launch traced here: 538 us
  other arithmetic  235 us (43%)
  matrix products  121 us (22%)
  starting transfers between devices  78.5 us (14%)
  waiting for transfers between devices  69.1 us (13%)
  between operations  22.1 us (4%)
  local copies, waits for them, and re-layouts  10.9 us (2%)
    another operation x35, other arithmetic, per_device(): factor = jnp.linalg.cholesky(gram_of(factor) + gram_of(partner))  173 us
    dot_general x32, matrix products, add_cell(): cell_terms = jnp.dot(pieces, cell_block, preferred_element_type=jnp.float32)  68.5 us
    ppermute x8, starting transfers between devices, extended_2(): lax.ppermute(head, axis, [((i + 1) % count, i) for i in range(ends)])  46.3 us
    all_gather x1, waiting for transfers between devices, per_device(): lax.all_gather(current.astype(jnp.bfloat16), 'orb', axis=0, tiled=True)  41.9 us
    dot_general x36, matrix products, spread_back(): lax.dot_general(three_parts(values), table, (((1,), (1,)), ((), ())), pre...  38.8 us
    another operation x6, other arithmetic, per_device(): factor = jnp.linalg.cholesky(gram_of(gathered))  33.9 us
    another operation x3, other arithmetic, forward_solve(): lax.linalg.triangular_solve(factor, values, left_side=True, lower=True)  19.7 us
    ppermute x5, starting transfers between devices, partner_2(): return lax.ppermute(value, axis, pairs)  16.8 us
  transfers between devices with their start and end apart: 22, of which 14 were waited for; matrix products, arithmetic and copies ran while one was open for 0% of the time, Pallas kernels for 0%

commit v1 on v0

--- a/solution.py
+++ b/solution.py
@@ -102,9 +102,16 @@
         previous, current = (current, following)
     block_rows = orbitals.shape[0]
     norm_scale = math.sqrt(orbitals.shape[1] * lax.axis_size("slab"))
-    gathered = lax.all_gather(current.astype(jnp.bfloat16), "orb", axis=0, tiled=True).astype(
-        current.dtype
-    )
+
+    def order_the_pieces_all(local, which_axis):
+        return jnp.concatenate(
+            lax.all_to_all(
+                jnp.stack([local] * lax.axis_size(which_axis), axis=0), which_axis, 0, 0
+            ),
+            axis=0,
+        )
+
+    gathered = order_the_pieces_all(current.astype(jnp.bfloat16), "orb").astype(current.dtype)
     factor = jnp.linalg.cholesky(gram_of(gathered))
     for level in range(lax.axis_size("slab").bit_length() - 1):
         partner = partner_2(factor.astype(jnp.bfloat16), "slab", level).astype(factor.dtype)

time: 549 us -> 529 us (0.964)
  the two profiles are of different devices: /device:TPU:2 before, /device:TPU:24 now
where the time goes in v1:
time: 529 us; the launch traced here: 518 us
  other arithmetic  235 us (44%)
  matrix products  120 us (23%)
  starting transfers between devices  81.7 us (15%)
  waiting for transfers between devices  59.6 us (11%)
  local copies, waits for them, and re-layouts  12.3 us (2%)
  between operations  8.91 us (2%)
    another operation x35, other arithmetic, per_device(): factor = jnp.linalg.cholesky(gram_of(factor) + gram_of(partner))  173 us
    dot_general x32, matrix products, add_cell(): cell_terms = jnp.dot(pieces, cell_block, preferred_element_type=jnp.float32)  68.5 us
    ppermute x8, starting transfers between devices, extended_2(): lax.ppermute(tail, axis, [(i, (i + 1) % count) for i in range(ends)])  41.7 us
    dot_general x36, matrix products, spread_back(): lax.dot_general(three_parts(values), table, (((1,), (1,)), ((), ())), pre...  38.8 us
    another operation x6, other arithmetic, per_device(): factor = jnp.linalg.cholesky(gram_of(gathered))  34 us
    all_to_all x1, waiting for transfers between devices, order_the_pieces_all(): lax.all_to_all(jnp.stack([local] * lax.axis_size(which_axis), axis=0), wh...  29.8 us
    another operation x3, other arithmetic, forward_solve(): lax.linalg.triangular_solve(factor, values, left_side=True, lower=True)  19.7 us
    ppermute x5, waiting for transfers between devices, partner_2(): return lax.ppermute(value, axis, pairs)  18.2 us
  transfers between devices with their start and end apart: 22, of which 14 were waited for; matrix products, arithmetic and copies ran while one was open for 0% of the time, Pallas kernels for 0%

profile of v1, /device:TPU:24, one launch (start us, length us, event | category | flops | bytes accessed | tf_op | source)
XLA Modules:
  0.0 518.5 jit_solution(1957067866903892398)
XLA Ops:
  9.5 33.1 %while.46 = (s32[]{:T(128)}, f32[32,2560]{1,0:T(8,128)S(1)}, s32[8,512]{1,0:T(8,128)}, bf16[32,2560]{1,0:T(8,128)(2,1)S(1)}, bf16[8,512,512]{2,1,0:T(8,128)(2,1)}, /*index=5*/s32[]{:T(128)}, s32[]{:T(128)}) while((s32[]{:T(128)}, f32[32,2560]{1,0:T(8,128)S(1)}, s32[8,512]{1,0:T(8,128)}, bf16[32,2560]{1,0:T(8,128)(2,1)S(1)}, ...), condition=%wide.region_1.2_spmd.clone, body=%wide.region_0.1_spmd.clone.sunk | while | flops 357007360 | bytes 3514971 | solution.py:83
  53.2 5.8 %collective-permute-start.4 = (bf16[32,256]{1,0:T(8,128)(2,1)S(1)}, bf16[32,256]{1,0:T(8,128)(2,1)S(1)}, u32[]{:S(2)}, u32[]{:S(2)}) collective-permute-start(bf16[32,256]{1,0:T(8,128)(2,1)S(1)} %get-tuple-element.342), channel_id=1, source_target_pairs={{0,8},{8,16},{16,24},{24,32},{32,40},{40,48},{48,56},{56,64},{64,7... | collective-permute-start | bytes 49160 | tf_op jit(solution)/shard_map/ppermute | solution.py:20
  62.4 27.5 %while.47 = (s32[]{:T(128)}, f32[32,2560]{1,0:T(8,128)S(1)}, s32[8,512]{1,0:T(8,128)S(1)}, bf16[32,2560]{1,0:T(8,128)(2,1)S(1)}, bf16[8,512,512]{2,1,0:T(8,128)(2,1)}, /*index=5*/s32[]{:T(128)}, s32[]{:T(128)}) while((s32[]{:T(128)}, f32[32,2560]{1,0:T(8,128)S(1)}, s32[8,512]{1,0:T(8,128)S(1)}, bf16[32,2560]{1,0:T(8,128)(2,1)S(1)}, ...), condition=%wide.region_3.4_spmd.clone, body=%wide.region_2.3_spmd.clone.sunk | while | flops 357007360 | bytes 3514971 | solution.py:83
  89.9 5.7 %collective-permute-start.6 = (f32[32,256]{1,0:T(8,128)S(1)}, f32[32,256]{1,0:T(8,128)S(1)}, u32[]{:S(2)}, u32[]{:S(2)}) collective-permute-start(f32[32,256]{1,0:T(8,128)S(1)} %get-tuple-element.299), channel_id=1, source_target_pairs={{0,8},{8,16},{16,24},{24,32},{32,40},{40,48},{48,56},{56,64},{64,7... | collective-permute-start | bytes 98312 | tf_op jit(solution)/shard_map/ppermute | solution.py:20
  101.0 5.8 %collective-permute-start.8 = (bf16[32,256]{1,0:T(8,128)(2,1)S(1)}, bf16[32,256]{1,0:T(8,128)(2,1)S(1)}, u32[]{:S(2)}, u32[]{:S(2)}) collective-permute-start(bf16[32,256]{1,0:T(8,128)(2,1)S(1)} %get-tuple-element.340), channel_id=1, source_target_pairs={{0,8},{8,16},{16,24},{24,32},{32,40},{40,48},{48,56},{56,64},{64,7... | collective-permute-start | bytes 49160 | tf_op jit(solution)/shard_map/ppermute | solution.py:20
  110.1 27.5 %while.48 = (s32[]{:T(128)}, f32[32,2560]{1,0:T(8,128)S(1)}, s32[8,512]{1,0:T(8,128)S(1)}, bf16[32,2560]{1,0:T(8,128)(2,1)S(1)}, bf16[8,512,512]{2,1,0:T(8,128)(2,1)}, /*index=5*/s32[]{:T(128)}, s32[]{:T(128)}) while((s32[]{:T(128)}, f32[32,2560]{1,0:T(8,128)S(1)}, s32[8,512]{1,0:T(8,128)S(1)}, bf16[32,2560]{1,0:T(8,128)(2,1)S(1)}, ...), condition=%wide.region_5.6_spmd.clone, body=%wide.region_4.5_spmd.clone.sunk | while | flops 357007360 | bytes 3514971 | solution.py:83
  148.7 5.8 %collective-permute-start.12 = (bf16[32,256]{1,0:T(8,128)(2,1)S(1)}, bf16[32,256]{1,0:T(8,128)(2,1)S(1)}, u32[]{:S(2)}, u32[]{:S(2)}) collective-permute-start(bf16[32,256]{1,0:T(8,128)(2,1)S(1)} %get-tuple-element.338), channel_id=1, source_target_pairs={{0,8},{8,16},{16,24},{24,32},{32,40},{40,48},{48,56},{56,64},{64,7... | collective-permute-start | bytes 49160 | tf_op jit(solution)/shard_map/ppermute | solution.py:20
  157.9 27.5 %while.49 = (s32[]{:T(128)}, f32[32,2560]{1,0:T(8,128)S(1)}, s32[8,512]{1,0:T(8,128)S(1)}, bf16[32,2560]{1,0:T(8,128)(2,1)S(1)}, bf16[8,512,512]{2,1,0:T(8,128)(2,1)}, /*index=5*/s32[]{:T(128)}, s32[]{:T(128)}) while((s32[]{:T(128)}, f32[32,2560]{1,0:T(8,128)S(1)}, s32[8,512]{1,0:T(8,128)S(1)}, bf16[32,2560]{1,0:T(8,128)(2,1)S(1)}, ...), condition=%wide.region_7.8_spmd.clone, body=%wide.region_6.7_spmd.clone.sunk | while | flops 357007360 | bytes 3514971 | solution.py:83
  185.4 5.7 %collective-permute-start.14 = (f32[32,256]{1,0:T(8,128)S(1)}, f32[32,256]{1,0:T(8,128)S(1)}, u32[]{:S(2)}, u32[]{:S(2)}) collective-permute-start(f32[32,256]{1,0:T(8,128)S(1)} %get-tuple-element.295), channel_id=1, source_target_pairs={{0,8},{8,16},{16,24},{24,32},{32,40},{40,48},{48,56},{56,64},{64,7... | collective-permute-start | bytes 98312 | tf_op jit(solution)/shard_map/ppermute | solution.py:20
  196.8 8.5 %all-to-all-start = ((bf16[8,32,2048]{2,1,0:T(8,128)(2,1)}), bf16[8,32,2048]{2,1,0:T(8,128)(2,1)S(1)}, u32[]{:S(2)}, u32[]{:S(2)}) async-start(bf16[8,32,2048]{2,1,0:T(8,128)(2,1)} %stack.2), calls=%async_computation | async-start | bytes 2097152 | tf_op jit(solution)/shard_map/all_to_all | solution.py:108
  205.2 29.8 %all-to-all-done = bf16[8,32,2048]{2,1,0:T(8,128)(2,1)S(1)} async-done(((bf16[8,32,2048]{2,1,0:T(8,128)(2,1)}), bf16[8,32,2048]{2,1,0:T(8,128)(2,1)S(1)}, u32[]{:S(2)}, u32[]{:S(2)}) %all-to-all-start) | async-done | bytes 1048608 | tf_op jit(solution)/shard_map/all_to_all | solution.py:108
  235.7 11.7 %cholesky.298 = f32[128,128]{1,0:T(8,128)S(1)} custom-call(f32[128,128]{1,0:T(8,128)S(1)} %cholesky.498), custom_call_target="Cholesky" | custom-call | tf_op jit(solution)/shard_map/jit(cholesky)/cholesky | solution.py:115
  247.5 9.8 %custom-call.21 = f32[1,128,128]{1,2,0:T(8,128)S(1)} custom-call(f32[1,128,128]{2,1,0:T(8,128)S(1)} %get-tuple-element.325), custom_call_target="InvertDiagBlocksLowerTriangular" | custom-call | tf_op jit(solution)/shard_map/jit(cholesky)/cholesky | solution.py:115
  257.8 11.7 %cholesky.315 = f32[128,128]{1,0:T(8,128)S(1)} custom-call(f32[128,128]{1,0:T(8,128)S(1)} %convolution_subtract_fusion.1), custom_call_target="Cholesky" | custom-call | tf_op jit(solution)/shard_map/jit(cholesky)/cholesky | solution.py:115
  271.5 8.6 %collective-permute-start.16 = (bf16[256,256]{1,0:T(8,128)(2,1)S(1)}, bf16[256,256]{1,0:T(8,128)(2,1)S(1)}, u32[]{:S(2)}, u32[]{:S(2)}) collective-permute-start(bf16[256,256]{1,0:T(8,128)(2,1)S(1)} %fusion.141), channel_id=1, source_target_pairs={{0,8},{8,0},{16,24},{24,16},{32,40},{40,32},{48,56},{56,48},{64,72... | collective-permute-start | bytes 393224 | tf_op jit(solution)/shard_map/ppermute | solution.py:32
  281.7 11.7 %cholesky.332 = f32[128,128]{1,0:T(8,128)S(1)} custom-call(f32[128,128]{1,0:T(8,128)S(1)} %cholesky.501), custom_call_target="Cholesky" | custom-call | tf_op jit(solution)/shard_map/jit(cholesky)/cholesky | solution.py:118
  293.5 9.8 %custom-call.22 = f32[1,128,128]{1,2,0:T(8,128)S(1)} custom-call(f32[1,128,128]{2,1,0:T(8,128)S(1)} %get-tuple-element.321), custom_call_target="InvertDiagBlocksLowerTriangular" | custom-call | tf_op jit(solution)/shard_map/jit(cholesky)/cholesky | solution.py:118
  303.7 11.7 %cholesky.349 = f32[128,128]{1,0:T(8,128)S(1)} custom-call(f32[128,128]{1,0:T(8,128)S(1)} %slice_subtract_fusion.4), custom_call_target="Cholesky" | custom-call | tf_op jit(solution)/shard_map/jit(cholesky)/cholesky | solution.py:118
  324.4 11.7 %cholesky.366 = f32[128,128]{1,0:T(8,128)S(1)} custom-call(f32[128,128]{1,0:T(8,128)S(1)} %cholesky.504), custom_call_target="Cholesky" | custom-call | tf_op jit(solution)/shard_map/jit(cholesky)/cholesky | solution.py:118
  336.2 9.8 %custom-call.23 = f32[1,128,128]{1,2,0:T(8,128)S(1)} custom-call(f32[1,128,128]{2,1,0:T(8,128)S(1)} %get-tuple-element.317), custom_call_target="InvertDiagBlocksLowerTriangular" | custom-call | tf_op jit(solution)/shard_map/jit(cholesky)/cholesky | solution.py:118
  346.5 11.7 %cholesky.383 = f32[128,128]{1,0:T(8,128)S(1)} custom-call(f32[128,128]{1,0:T(8,128)S(1)} %slice_subtract_fusion.3), custom_call_target="Cholesky" | custom-call | tf_op jit(solution)/shard_map/jit(cholesky)/cholesky | solution.py:118
  361.8 6.0 %collective-permute-done.18 = bf16[256,256]{1,0:T(8,128)(2,1)S(1)} collective-permute-done((bf16[256,256]{1,0:T(8,128)(2,1)S(1)}, bf16[256,256]{1,0:T(8,128)(2,1)S(1)}, u32[]{:S(2)}, u32[]{:S(2)}) %collective-permute-start.18) | collective-permute-done | bytes 131104 | tf_op jit(solution)/shard_map/ppermute | solution.py:32
  368.3 11.7 %cholesky.400 = f32[128,128]{1,0:T(8,128)S(1)} custom-call(f32[128,128]{1,0:T(8,128)S(1)} %cholesky.507), custom_call_target="Cholesky" | custom-call | tf_op jit(solution)/shard_map/jit(cholesky)/cholesky | solution.py:118
  380.1 9.8 %custom-call.24 = f32[1,128,128]{1,2,0:T(8,128)S(1)} custom-call(f32[1,128,128]{2,1,0:T(8,128)S(1)} %get-tuple-element.313), custom_call_target="InvertDiagBlocksLowerTriangular" | custom-call | tf_op jit(solution)/shard_map/jit(cholesky)/cholesky | solution.py:118
  390.4 11.7 %cholesky.417 = f32[128,128]{1,0:T(8,128)S(1)} custom-call(f32[128,128]{1,0:T(8,128)S(1)} %slice_subtract_fusion.2), custom_call_target="Cholesky" | custom-call | tf_op jit(solution)/shard_map/jit(cholesky)/cholesky | solution.py:118
  410.4 11.7 %cholesky.434 = f32[128,128]{1,0:T(8,128)S(1)} custom-call(f32[128,128]{1,0:T(8,128)S(1)} %cholesky.510), custom_call_target="Cholesky" | custom-call | tf_op jit(solution)/shard_map/jit(cholesky)/cholesky | solution.py:118
  422.2 9.8 %custom-call.25 = f32[1,128,128]{1,2,0:T(8,128)S(1)} custom-call(f32[1,128,128]{2,1,0:T(8,128)S(1)} %get-tuple-element.309), custom_call_target="InvertDiagBlocksLowerTriangular" | custom-call | tf_op jit(solution)/shard_map/jit(cholesky)/cholesky | solution.py:118
  432.5 11.7 %cholesky.451 = f32[128,128]{1,0:T(8,128)S(1)} custom-call(f32[128,128]{1,0:T(8,128)S(1)} %slice_subtract_fusion.1), custom_call_target="Cholesky" | custom-call | tf_op jit(solution)/shard_map/jit(cholesky)/cholesky | solution.py:118
  454.0 11.7 %cholesky.468 = f32[128,128]{1,0:T(8,128)S(1)} custom-call(f32[128,128]{1,0:T(8,128)S(1)} %cholesky.513), custom_call_target="Cholesky" | custom-call | tf_op jit(solution)/shard_map/jit(cholesky)/cholesky | solution.py:118
  465.8 9.8 %custom-call.26 = f32[1,128,128]{1,2,0:T(8,128)S(1)} custom-call(f32[1,128,128]{2,1,0:T(8,128)S(1)} %get-tuple-element.305), custom_call_target="InvertDiagBlocksLowerTriangular" | custom-call | tf_op jit(solution)/shard_map/jit(cholesky)/cholesky | solution.py:118
  476.1 11.7 %cholesky.485 = f32[128,128]{1,0:T(8,128)S(1)} custom-call(f32[128,128]{1,0:T(8,128)S(1)} %slice_subtract_fusion), custom_call_target="Cholesky" | custom-call | tf_op jit(solution)/shard_map/jit(cholesky)/cholesky | solution.py:118
  494.9 19.7 %custom-call.11 = f32[2,128,128]{1,2,0:T(8,128)S(1)} custom-call(f32[2,128,128]{2,1,0:T(8,128)S(1)} %get-tuple-element.145), custom_call_target="InvertDiagBlocksLowerTriangular" | custom-call | tf_op jit(solution)/shard_map/triangular_solve | solution.py:46
  (301 shorter events, 211.7 us)
Async XLA Ops:
  2.5 5.6 %collective-permute-start = (bf16[32,256]{1,0:T(8,128)(2,1)S(1)}, bf16[32,256]{1,0:T(8,128)(2,1)S(1)}, u32[]{:S(2)}, u32[]{:S(2)}) collective-permute-start(bf16[32,256]{1,0:T(8,128)(2,1)S(1)} %get-tuple-element.344), channel_id=1, source_target_pairs={{0,8},{8,16},{16,24},{24,32},{32,40},{40,48},{48,56},{56,64},{64,7... | collective-permute-start | bytes 49160 | tf_op jit(solution)/shard_map/ppermute | solution.py:20
  4.4 5.1 collective-permute-start.1
  42.6 19.7 %copy-start.1 = (s32[8,512]{1,0:T(8,128)S(1)}, s32[8,512]{1,0:T(8,128)}, u32[]{:S(2)}) copy-start(s32[8,512]{1,0:T(8,128)} %get-tuple-element.648) | copy-start | bytes 49156
  42.6 7.2 %collective-permute-start.2 = (f32[32,256]{1,0:T(8,128)S(1)}, f32[32,256]{1,0:T(8,128)S(1)}, u32[]{:S(2)}, u32[]{:S(2)}) collective-permute-start(f32[32,256]{1,0:T(8,128)S(1)} %get-tuple-element.301), channel_id=1, source_target_pairs={{0,8},{8,16},{16,24},{24,32},{32,40},{40,48},{48,56},{56,64},{64,7... | collective-permute-start | bytes 98312 | tf_op jit(solution)/shard_map/ppermute | solution.py:20
  47.9 3.5 collective-permute-start.3
  53.2 7.7 %collective-permute-start.4 = (bf16[32,256]{1,0:T(8,128)(2,1)S(1)}, bf16[32,256]{1,0:T(8,128)(2,1)S(1)}, u32[]{:S(2)}, u32[]{:S(2)}) collective-permute-start(bf16[32,256]{1,0:T(8,128)(2,1)S(1)} %get-tuple-element.342), channel_id=1, source_target_pairs={{0,8},{8,16},{16,24},{24,32},{32,40},{40,48},{48,56},{56,64},{64,7... | collective-permute-start | bytes 49160 | tf_op jit(solution)/shard_map/ppermute | solution.py:20
  59.0 3.4 collective-permute-start.5
  62.4 37.7 %copy-start = (f32[32,2048]{1,0:T(8,128)S(1)}, f32[32,2048]{1,0:T(8,128)}, u32[]{:S(2)}) copy-start(f32[32,2048]{1,0:T(8,128)} %param.14) | copy-start | bytes 786436
  89.9 7.7 %collective-permute-start.6 = (f32[32,256]{1,0:T(8,128)S(1)}, f32[32,256]{1,0:T(8,128)S(1)}, u32[]{:S(2)}, u32[]{:S(2)}) collective-permute-start(f32[32,256]{1,0:T(8,128)S(1)} %get-tuple-element.299), channel_id=1, source_target_pairs={{0,8},{8,16},{16,24},{24,32},{32,40},{40,48},{48,56},{56,64},{64,7... | collective-permute-start | bytes 98312 | tf_op jit(solution)/shard_map/ppermute | solution.py:20
  95.6 3.5 collective-permute-start.7
  101.0 7.7 %collective-permute-start.8 = (bf16[32,256]{1,0:T(8,128)(2,1)S(1)}, bf16[32,256]{1,0:T(8,128)(2,1)S(1)}, u32[]{:S(2)}, u32[]{:S(2)}) collective-permute-start(bf16[32,256]{1,0:T(8,128)(2,1)S(1)} %get-tuple-element.340), channel_id=1, source_target_pairs={{0,8},{8,16},{16,24},{24,32},{32,40},{40,48},{48,56},{56,64},{64,7... | collective-permute-start | bytes 49160 | tf_op jit(solution)/shard_map/ppermute | solution.py:20
  106.8 3.4 collective-permute-start.9
  137.6 7.9 %collective-permute-start.10 = (f32[32,256]{1,0:T(8,128)S(1)}, f32[32,256]{1,0:T(8,128)S(1)}, u32[]{:S(2)}, u32[]{:S(2)}) collective-permute-start(f32[32,256]{1,0:T(8,128)S(1)} %get-tuple-element.297), channel_id=1, source_target_pairs={{0,8},{8,16},{16,24},{24,32},{32,40},{40,48},{48,56},{56,64},{64,7... | collective-permute-start | bytes 98312 | tf_op jit(solution)/shard_map/ppermute | solution.py:20
  143.4 3.5 collective-permute-start.11
  148.7 7.7 %collective-permute-start.12 = (bf16[32,256]{1,0:T(8,128)(2,1)S(1)}, bf16[32,256]{1,0:T(8,128)(2,1)S(1)}, u32[]{:S(2)}, u32[]{:S(2)}) collective-permute-start(bf16[32,256]{1,0:T(8,128)(2,1)S(1)} %get-tuple-element.338), channel_id=1, source_target_pairs={{0,8},{8,16},{16,24},{24,32},{32,40},{40,48},{48,56},{56,64},{64,7... | collective-permute-start | bytes 49160 | tf_op jit(solution)/shard_map/ppermute | solution.py:20
  154.5 3.4 collective-permute-start.13
  185.4 7.7 %collective-permute-start.14 = (f32[32,256]{1,0:T(8,128)S(1)}, f32[32,256]{1,0:T(8,128)S(1)}, u32[]{:S(2)}, u32[]{:S(2)}) collective-permute-start(f32[32,256]{1,0:T(8,128)S(1)} %get-tuple-element.295), channel_id=1, source_target_pairs={{0,8},{8,16},{16,24},{24,32},{32,40},{40,48},{48,56},{56,64},{64,7... | collective-permute-start | bytes 98312 | tf_op jit(solution)/shard_map/ppermute | solution.py:20
  191.1 3.5 collective-permute-start.15
  196.8 38.3 %all-to-all-start = ((bf16[8,32,2048]{2,1,0:T(8,128)(2,1)}), bf16[8,32,2048]{2,1,0:T(8,128)(2,1)S(1)}, u32[]{:S(2)}, u32[]{:S(2)}) async-start(bf16[8,32,2048]{2,1,0:T(8,128)(2,1)} %stack.2), calls=%async_computation | async-start | bytes 2097152 | tf_op jit(solution)/shard_map/all_to_all | solution.py:108
  271.5 9.7 %collective-permute-start.16 = (bf16[256,256]{1,0:T(8,128)(2,1)S(1)}, bf16[256,256]{1,0:T(8,128)(2,1)S(1)}, u32[]{:S(2)}, u32[]{:S(2)}) collective-permute-start(bf16[256,256]{1,0:T(8,128)(2,1)S(1)} %fusion.141), channel_id=1, source_target_pairs={{0,8},{8,0},{16,24},{24,16},{32,40},{40,32},{48,56},{56,48},{64,72... | collective-permute-start | bytes 393224 | tf_op jit(solution)/shard_map/ppermute | solution.py:32
  318.1 5.9 %collective-permute-start.17 = (bf16[256,256]{1,0:T(8,128)(2,1)S(1)}, bf16[256,256]{1,0:T(8,128)(2,1)S(1)}, u32[]{:S(2)}, u32[]{:S(2)}) collective-permute-start(bf16[256,256]{1,0:T(8,128)(2,1)S(1)} %fusion.143), channel_id=1, source_target_pairs={{0,16},{8,24},{16,0},{24,8},{32,48},{40,56},{48,32},{56,40},{64,80... | collective-permute-start | bytes 393224 | tf_op jit(solution)/shard_map/ppermute | solution.py:32
  360.9 7.0 %collective-permute-start.18 = (bf16[256,256]{1,0:T(8,128)(2,1)S(1)}, bf16[256,256]{1,0:T(8,128)(2,1)S(1)}, u32[]{:S(2)}, u32[]{:S(2)}) collective-permute-start(bf16[256,256]{1,0:T(8,128)(2,1)S(1)} %fusion.145), channel_id=1, source_target_pairs={{0,32},{8,40},{16,48},{24,56},{32,0},{40,8},{48,16},{56,24},{64,96... | collective-permute-start | bytes 393224 | tf_op jit(solution)/shard_map/ppermute | solution.py:32
  404.7 5.2 %collective-permute-start.19 = (bf16[256,256]{1,0:T(8,128)(2,1)S(1)}, bf16[256,256]{1,0:T(8,128)(2,1)S(1)}, u32[]{:S(2)}, u32[]{:S(2)}) collective-permute-start(bf16[256,256]{1,0:T(8,128)(2,1)S(1)} %fusion.147), channel_id=1, source_target_pairs={{0,64},{8,72},{16,80},{24,88},{32,96},{40,104},{48,112},{56,120},{... | collective-permute-start | bytes 393224 | tf_op jit(solution)/shard_map/ppermute | solution.py:32
  446.9 6.8 %collective-permute-start.20 = (bf16[256,256]{1,0:T(8,128)(2,1)S(1)}, bf16[256,256]{1,0:T(8,128)(2,1)S(1)}, u32[]{:S(2)}, u32[]{:S(2)}) collective-permute-start(bf16[256,256]{1,0:T(8,128)(2,1)S(1)} %fusion.149), channel_id=1, source_target_pairs={{0,128},{8,136},{16,144},{24,152},{32,160},{40,168},{48,176},{56,1... | collective-permute-start | bytes 393224 | tf_op jit(solution)/shard_map/ppermute | solution.py:32
